TPU v7x, 32 devices: a whole 2x2x4 slice. The times are simulated.
32 devices in a mesh: section: 4 (over z), dp: 8 (over y, x, core).
Axes of the slice: x: 2, y: 2, z: 4, core: 2. Of those that a mesh axis runs over, the one named last changes fastest.
Arguments:
- acts: bfloat16 [4, 4, 8, 12, 16, 512], P('section', None, 'dp'), may hold values from -6 to 6
- out_grad: bfloat16 [4, 8, 12, 16, 512], P(None, 'dp'), may hold values from -6 to 6
- depth_kernel: bfloat16 [4, 3, 3, 512], P('section'), may hold values from -2 to 2
- point_weight: bfloat16 [4, 512, 512], P('section'), may hold values from -0.25 to 0.25
- bn_gain: float32 [4, 512], P('section'), may hold values from 0.15 to 0.45
Outputs:
- act_grad: bfloat16 [4, 4, 8, 12, 16, 512], P('section', None, 'dp')
- point_grad: float32 [4, 512, 512], P('section')
- kernel_grad: float32 [4, 3, 3, 512], P('section')
- gain_grad: float32 [4, 512], P('section')
- bias_grad: float32 [4, 512], P('section')
All inputs are finite; a program needn't handle non-finite values.
Results may differ from a plain program's by a relative error of at most 0.025.
Values may be sent and summed in bfloat16 or wider, within the bound.
No kernel may reach another device: no remote copies, remote signals or barrier semaphores. Data moves between devices by JAX's collectives and lax.ppermute only.
A program may use at most 64 MiB of HBM per device.

v0:
```python
import jax
import jax.numpy as jnp
from jax import lax
from jax.sharding import PartitionSpec as P

epsilon = 1e-05


def shifted(x, axis, by):
    length = lax.axis_size(axis)
    pairs = [(i, i + by) for i in range(length) if 0 <= i + by < length]
    return lax.ppermute(x, axis, pairs)


def depthwise(active, kernel):
    padded = jnp.pad(active, ((0, 0), (1, 1), (1, 1), (0, 0)))
    height, width = (active.shape[1], active.shape[2])
    summed = jnp.zeros(active.shape, jnp.float32)
    for row_off in range(3):
        for col_off in range(3):
            summed = (
                summed
                + kernel[row_off, col_off]
                * padded[:, row_off : row_off + height, col_off : col_off + width]
            )
    return summed


def depthwise_back(grad, kernel):
    padded = jnp.pad(grad, ((0, 0), (1, 1), (1, 1), (0, 0)))
    height, width = (grad.shape[1], grad.shape[2])
    summed = jnp.zeros(grad.shape, jnp.float32)
    for row_off in range(3):
        for col_off in range(3):
            summed = (
                summed
                + kernel[row_off, col_off]
                * padded[:, 2 - row_off : 2 - row_off + height, 2 - col_off : 2 - col_off + width]
            )
    return summed


def kernel_terms(active, grad):
    padded = jnp.pad(active, ((0, 0), (1, 1), (1, 1), (0, 0)))
    height, width = (active.shape[1], active.shape[2])
    table = []
    for row_off in range(3):
        line = []
        for col_off in range(3):
            line.append(
                jnp.sum(
                    padded[:, row_off : row_off + height, col_off : col_off + width] * grad,
                    axis=(0, 1, 2),
                )
            )
        table.append(jnp.stack(line))
    return jnp.stack(table)


def pick(array, slot):
    return lax.dynamic_index_in_dim(array, slot, 0, keepdims=False)


def body(acts, out_grad, depth_kernel, point_weight, bn_gain):
    sections = lax.axis_size("section")
    replicas = lax.axis_size("dp")
    my_section = lax.axis_index("section")
    micros, images, height, width, channels = acts.shape[1:]
    rows = images * height * width
    count = images * replicas * height * width
    shape = (images, height, width, channels)
    inputs = acts[0]
    kernel = depth_kernel[0].astype(jnp.float32)
    weight = point_weight[0]
    gain = bn_gain[0]
    active = jnp.maximum(inputs.astype(jnp.float32), 0.0)
    depth_out = depthwise(active.reshape(micros * images, height, width, channels), kernel).astype(
        jnp.bfloat16
    )
    depth_flat = depth_out.reshape(micros * rows, channels)
    pre_norm = jnp.dot(depth_flat, weight, preferred_element_type=jnp.float32).reshape(
        micros, rows, channels
    )
    center_sum, square_sum = lax.psum(
        (jnp.sum(pre_norm, axis=1), jnp.sum(pre_norm * pre_norm, axis=1)), "dp"
    )
    center_all = center_sum / count
    inv_all = lax.rsqrt(square_sum / count - center_all * center_all + epsilon)
    normed_all = (pre_norm - center_all[:, None, :]) * inv_all[:, None, :]
    pre_bank = jnp.zeros((micros, rows, channels), jnp.bfloat16)
    depth_bank = jnp.zeros((micros,) + shape, jnp.float32)

    def step(turn, carry):
        incoming, grads_out, gain_acc, bias_acc, point_acc, kernel_acc, pre_store, depth_store = (
            carry
        )
        micro = turn - (sections - 1 - my_section)
        valid = jnp.logical_and(micro >= 0, micro < micros)
        slot = jnp.clip(micro, 0, micros - 1)
        flag = valid.astype(jnp.float32)
        upstream = jnp.where(my_section == sections - 1, pick(out_grad, slot), incoming)
        upstream = upstream.astype(jnp.float32).reshape(rows, channels)
        normed = pick(normed_all, slot)
        inv_std = pick(inv_all, slot)
        sum_grad, sum_cross = lax.psum(
            (jnp.sum(upstream, axis=0), jnp.sum(upstream * normed, axis=0)), "dp"
        )
        pre_grad = (
            gain * inv_std * (upstream - sum_grad / count - normed * sum_cross / count)
        ).astype(jnp.bfloat16)
        depth_grad = lax.dot_general(
            pre_grad, weight, (((1,), (1,)), ((), ())), preferred_element_type=jnp.float32
        ).reshape(shape)
        input_slot = pick(inputs, slot)
        back = depthwise_back(depth_grad, kernel)
        input_grad = (upstream.reshape(shape) + jnp.where(input_slot > 0, back, 0.0)).astype(
            jnp.bfloat16
        )
        gain_acc = gain_acc + flag * sum_cross
        bias_acc = bias_acc + flag * sum_grad
        kept_pre = jnp.where(valid, pre_grad, pick(pre_store, slot))
        pre_store = lax.dynamic_update_index_in_dim(pre_store, kept_pre, slot, 0)
        kept_depth = jnp.where(valid, depth_grad, pick(depth_store, slot))
        depth_store = lax.dynamic_update_index_in_dim(depth_store, kept_depth, slot, 0)
        kept_grad = jnp.where(valid, input_grad, pick(grads_out, slot))
        grads_out = lax.dynamic_update_index_in_dim(grads_out, kept_grad, slot, 0)
        incoming = shifted(input_grad, "section", -1)
        return (
            incoming,
            grads_out,
            gain_acc,
            bias_acc,
            point_acc,
            kernel_acc,
            pre_store,
            depth_store,
        )

    start = (
        jnp.zeros(shape, jnp.bfloat16),
        jnp.zeros((micros,) + shape, jnp.bfloat16),
        jnp.zeros((channels,), jnp.float32),
        jnp.zeros((channels,), jnp.float32),
        jnp.zeros((channels, channels), jnp.float32),
        jnp.zeros((3, 3, channels), jnp.float32),
        pre_bank,
        depth_bank,
    )
    final = lax.fori_loop(0, sections + micros - 1, step, start)
    grads_out, gain_acc, bias_acc, point_acc, kernel_acc, pre_store, depth_store = final[1:]
    point_acc = lax.dot_general(
        depth_flat,
        pre_store.reshape(micros * rows, channels),
        (((0,), (0,)), ((), ())),
        preferred_element_type=jnp.float32,
    )
    kernel_acc = kernel_terms(
        active.reshape(micros * images, height, width, channels),
        depth_store.reshape(micros * images, height, width, channels),
    )
    point_sum, kernel_sum = (
        lax.psum(point_acc.astype(jnp.bfloat16), "dp").astype(jnp.float32),
        lax.psum(kernel_acc.astype(jnp.bfloat16), "dp").astype(jnp.float32),
    )
    return (grads_out[None], point_sum[None], kernel_sum[None], gain_acc[None], bias_acc[None])


def solution(mesh):
    return jax.shard_map(
        body,
        mesh=mesh,
        in_specs=(
            P("section", None, "dp", None, None, None),
            P(None, "dp", None, None, None),
            P("section", None, None, None),
            P("section", None, None),
            P("section", None),
        ),
        out_specs=(
            P("section", None, "dp", None, None, None),
            P("section", None, None),
            P("section", None, None, None),
            P("section", None),
            P("section", None),
        ),
        check_vma=False,
    )
```

profile of v0, /device:TPU:0, one launch (start us, length us, event | category | flops | bytes accessed | tf_op | source)
XLA Modules:
  0.0 283.1 jit_solution(14415372862434217522)
XLA Ops:
  9.3 2.2 add_convert_fusion
  13.3 25.5 %all-reduce.3 = (f32[4,512]{1,0:T(4,128)S(1)}, f32[4,512]{1,0:T(4,128)S(1)}) all-reduce(f32[4,512]{1,0:T(4,128)S(1)} %get-tuple-element.436, f32[4,512]{1,0:T(4,128)S(1)} %get-tuple-element.435), channel_id=1, replica_groups=mesh['section'=4,'dp'=8] {'dp'}, use_global_device_ids=true, to_apply=%region_3.4 | all-reduce | flops 4096 | bytes 32768 | tf_op jit(solution)/shard_map/psum | solution.py:84
  43.9 174.0 %while.26 = (s32[]{:T(128)}, bf16[1,12,16,512]{3,2,1,0:T(8,128)(2,1)S(1)}, bf16[4,1,12,16,512]{4,3,2,1,0:T(8,128)(2,1)}, f32[512]{0:T(512)S(1)}, f32[512]{0:T(51...) while((s32[]{:T(128)}, ...), condition=%wide.region_9.10_spmd.clone, body=%wide.region_4.9_spmd.clone.sunk | while | flops 105189384 | bytes 8489298 | solution.py:149
  46.0 11.8 %all-reduce.5 = (f32[512]{0:T(512)S(1)}, f32[512]{0:T(512)S(1)}) all-reduce(f32[512]{0:T(512)S(1)} %get-tuple-element.621, f32[512]{0:T(512)S(1)} %get-tuple-element.622), channel_id=1, replica_groups=mesh['section'=4,'dp'=8] {'dp'}, use_global_device_ids=true, to_apply=%region_8.8 | all-reduce | flops 1024 | bytes 8192 | tf_op jit(solution)/shard_map/while/body/eval_jaxpr/psum | solution.py:105
  58.2 2.0 bitcast_dynamic-update-slice_fusion.2
  65.0 3.7 %collective-permute-done = bf16[1,12,16,512]{3,2,1,0:T(8,128)(2,1)S(1)} collective-permute-done((bf16[1,12,16,512]{3,2,1,0:T(8,128)(2,1)S(1)}, bf16[1,12,16,512]{3,2,1,0:T(8,128)(2,1)S(1)}, u32[]{:S(2)}, u32[]{:S(2)}) %collective-permute-start) | collective-permute-done | bytes 196640 | tf_op jit(solution)/shard_map/while/body/eval_jaxpr/ppermute | solution.py:12
  70.8 11.8 %all-reduce.5 = (f32[512]{0:T(512)S(1)}, f32[512]{0:T(512)S(1)}) all-reduce(f32[512]{0:T(512)S(1)} %get-tuple-element.621, f32[512]{0:T(512)S(1)} %get-tuple-element.622), channel_id=1, replica_groups=mesh['section'=4,'dp'=8] {'dp'}, use_global_device_ids=true, to_apply=%region_8.8 | all-reduce | flops 1024 | bytes 8192 | tf_op jit(solution)/shard_map/while/body/eval_jaxpr/psum | solution.py:105
  89.8 3.7 %collective-permute-done = bf16[1,12,16,512]{3,2,1,0:T(8,128)(2,1)S(1)} collective-permute-done((bf16[1,12,16,512]{3,2,1,0:T(8,128)(2,1)S(1)}, bf16[1,12,16,512]{3,2,1,0:T(8,128)(2,1)S(1)}, u32[]{:S(2)}, u32[]{:S(2)}) %collective-permute-start) | collective-permute-done | bytes 196640 | tf_op jit(solution)/shard_map/while/body/eval_jaxpr/ppermute | solution.py:12
  95.7 11.8 %all-reduce.5 = (f32[512]{0:T(512)S(1)}, f32[512]{0:T(512)S(1)}) all-reduce(f32[512]{0:T(512)S(1)} %get-tuple-element.621, f32[512]{0:T(512)S(1)} %get-tuple-element.622), channel_id=1, replica_groups=mesh['section'=4,'dp'=8] {'dp'}, use_global_device_ids=true, to_apply=%region_8.8 | all-reduce | flops 1024 | bytes 8192 | tf_op jit(solution)/shard_map/while/body/eval_jaxpr/psum | solution.py:105
  107.9 2.0 bitcast_dynamic-update-slice_fusion.2
  114.7 3.7 %collective-permute-done = bf16[1,12,16,512]{3,2,1,0:T(8,128)(2,1)S(1)} collective-permute-done((bf16[1,12,16,512]{3,2,1,0:T(8,128)(2,1)S(1)}, bf16[1,12,16,512]{3,2,1,0:T(8,128)(2,1)S(1)}, u32[]{:S(2)}, u32[]{:S(2)}) %collective-permute-start) | collective-permute-done | bytes 196640 | tf_op jit(solution)/shard_map/while/body/eval_jaxpr/ppermute | solution.py:12
  120.5 11.8 %all-reduce.5 = (f32[512]{0:T(512)S(1)}, f32[512]{0:T(512)S(1)}) all-reduce(f32[512]{0:T(512)S(1)} %get-tuple-element.621, f32[512]{0:T(512)S(1)} %get-tuple-element.622), channel_id=1, replica_groups=mesh['section'=4,'dp'=8] {'dp'}, use_global_device_ids=true, to_apply=%region_8.8 | all-reduce | flops 1024 | bytes 8192 | tf_op jit(solution)/shard_map/while/body/eval_jaxpr/psum | solution.py:105
  139.5 3.7 %collective-permute-done = bf16[1,12,16,512]{3,2,1,0:T(8,128)(2,1)S(1)} collective-permute-done((bf16[1,12,16,512]{3,2,1,0:T(8,128)(2,1)S(1)}, bf16[1,12,16,512]{3,2,1,0:T(8,128)(2,1)S(1)}, u32[]{:S(2)}, u32[]{:S(2)}) %collective-permute-start) | collective-permute-done | bytes 196640 | tf_op jit(solution)/shard_map/while/body/eval_jaxpr/ppermute | solution.py:12
  145.4 11.8 %all-reduce.5 = (f32[512]{0:T(512)S(1)}, f32[512]{0:T(512)S(1)}) all-reduce(f32[512]{0:T(512)S(1)} %get-tuple-element.621, f32[512]{0:T(512)S(1)} %get-tuple-element.622), channel_id=1, replica_groups=mesh['section'=4,'dp'=8] {'dp'}, use_global_device_ids=true, to_apply=%region_8.8 | all-reduce | flops 1024 | bytes 8192 | tf_op jit(solution)/shard_map/while/body/eval_jaxpr/psum | solution.py:105
  164.4 3.7 %collective-permute-done = bf16[1,12,16,512]{3,2,1,0:T(8,128)(2,1)S(1)} collective-permute-done((bf16[1,12,16,512]{3,2,1,0:T(8,128)(2,1)S(1)}, bf16[1,12,16,512]{3,2,1,0:T(8,128)(2,1)S(1)}, u32[]{:S(2)}, u32[]{:S(2)}) %collective-permute-start) | collective-permute-done | bytes 196640 | tf_op jit(solution)/shard_map/while/body/eval_jaxpr/ppermute | solution.py:12
  170.2 11.8 %all-reduce.5 = (f32[512]{0:T(512)S(1)}, f32[512]{0:T(512)S(1)}) all-reduce(f32[512]{0:T(512)S(1)} %get-tuple-element.621, f32[512]{0:T(512)S(1)} %get-tuple-element.622), channel_id=1, replica_groups=mesh['section'=4,'dp'=8] {'dp'}, use_global_device_ids=true, to_apply=%region_8.8 | all-reduce | flops 1024 | bytes 8192 | tf_op jit(solution)/shard_map/while/body/eval_jaxpr/psum | solution.py:105
  189.2 3.7 %collective-permute-done = bf16[1,12,16,512]{3,2,1,0:T(8,128)(2,1)S(1)} collective-permute-done((bf16[1,12,16,512]{3,2,1,0:T(8,128)(2,1)S(1)}, bf16[1,12,16,512]{3,2,1,0:T(8,128)(2,1)S(1)}, u32[]{:S(2)}, u32[]{:S(2)}) %collective-permute-start) | collective-permute-done | bytes 196640 | tf_op jit(solution)/shard_map/while/body/eval_jaxpr/ppermute | solution.py:12
  195.1 11.8 %all-reduce.5 = (f32[512]{0:T(512)S(1)}, f32[512]{0:T(512)S(1)}) all-reduce(f32[512]{0:T(512)S(1)} %get-tuple-element.621, f32[512]{0:T(512)S(1)} %get-tuple-element.622), channel_id=1, replica_groups=mesh['section'=4,'dp'=8] {'dp'}, use_global_device_ids=true, to_apply=%region_8.8 | all-reduce | flops 1024 | bytes 8192 | tf_op jit(solution)/shard_map/while/body/eval_jaxpr/psum | solution.py:105
  214.1 3.7 %collective-permute-done = bf16[1,12,16,512]{3,2,1,0:T(8,128)(2,1)S(1)} collective-permute-done((bf16[1,12,16,512]{3,2,1,0:T(8,128)(2,1)S(1)}, bf16[1,12,16,512]{3,2,1,0:T(8,128)(2,1)S(1)}, u32[]{:S(2)}, u32[]{:S(2)}) %collective-permute-start) | collective-permute-done | bytes 196640 | tf_op jit(solution)/shard_map/while/body/eval_jaxpr/ppermute | solution.py:12
  217.8 2.9 %fusion.37 = bf16[1,512,512]{2,1,0:T(8,128)(2,1)} fusion(bf16[768,512]{1,0:T(8,128)(2,1)} %bitcast.175, bf16[768,512]{1,0:T(8,128)(2,1)} %bitcast.173), kind=kOutput, calls=%fused_computation.83 | convolution fusion | flops 402915328 | bytes 2097152 | tf_op jit(solution)/shard_map/dot_general | solution.py:151
  220.8 6.4 %fusion.28 = (bf16[512]{0:T(512)(128)(2,1)S(1)}, bf16[512]{0:T(512)(128)(2,1)S(1)}, bf16[512]{0:T(512)(128)(2,1)S(1)}, bf16[512]{0:T(512)(128)(2,1)S(1)}, bf16[5...) fusion(f32[4,1,12,16,512]{4,3,2,1,0:T(8,128)S(1)} %copy-done, ...), kind=kLoop, calls=%fused_computation.69 | loop fusion | flops 7859712 | bytes 3941376 | tf_op jit(solution)/shard_map/reduce_sum | solution.py:51
  227.4 22.5 %psum.59 = bf16[1,3,3,512]{3,0,2,1:T(2,128)(2,1)S(1)} all-reduce(bf16[1,3,3,512]{3,0,2,1:T(2,128)(2,1)S(1)} %broadcast_in_dim.73), channel_id=1, replica_groups=mesh['section'=4,'dp'=8] {'dp'}, use_global_device_ids=true, to_apply=%region_20.21 | all-reduce | flops 4608 | bytes 18432 | tf_op jit(solution)/shard_map/psum | solution.py:163
  250.6 23.5 %all-reduce.8.cloned.1.call-done = bf16[1,512,512]{2,1,0:T(8,128)(2,1)} async-done(((bf16[1,512,512]{2,1,0:T(8,128)(2,1)}), bf16[1,512,512]{2,1,0:T(8,128)(2,1)}) %all-reduce.8.cloned.1.call-update) | async-done | bytes 524304 | tf_op jit(solution)/shard_map/psum | solution.py:162
  274.1 2.1 broadcast_in_dim.72
  (133 shorter events, 70.6 us)
Async XLA Ops:
  7.2 266.9 %all-reduce.8.cloned.1.call-start = ((), (), s32[]{:S(2)}) async-start(), calls=%async_computation | async-start | bytes 1048576 | tf_op jit(solution)/shard_map/psum | solution.py:162
  9.3 4.0 %copy-start.1 = (f32[4,12,16,512]{3,2,1,0:T(8,128)}, f32[4,12,16,512]{3,2,1,0:T(8,128)S(1)}, u32[]{:S(2)}) copy-start(f32[4,12,16,512]{3,2,1,0:T(8,128)S(1)} %maximum_bitcast_fusion) | copy-start | bytes 4718596
  9.3 2.2 copy-start.2
  11.6 1.8 copy-start.4
  40.6 3.3 %copy-start.6 = (f32[1,512]{1,0:T(1,128)S(1)}, f32[1,512]{1,0:T(1,128)}, u32[]{:S(2)}) copy-start(f32[1,512]{1,0:T(1,128)} %param.11) | copy-start | bytes 6148
  60.2 8.6 %collective-permute-start = (bf16[1,12,16,512]{3,2,1,0:T(8,128)(2,1)S(1)}, bf16[1,12,16,512]{3,2,1,0:T(8,128)(2,1)S(1)}, u32[]{:S(2)}, u32[]{:S(2)}) collective-permute-start(bf16[1,12,16,512]{3,2,1,0:T(8,128)(2,1)S(1)} %get-tuple-element.631), channel_id=1, source_target_pairs={{8,0},{16,8},{24,16},{9,1},{17,9},{25,17},{10,2},{18,10},{26,18},{... | collective-permute-start | bytes 589832 | tf_op jit(solution)/shard_map/while/body/eval_jaxpr/ppermute | solution.py:12
  85.0 8.6 %collective-permute-start = (bf16[1,12,16,512]{3,2,1,0:T(8,128)(2,1)S(1)}, bf16[1,12,16,512]{3,2,1,0:T(8,128)(2,1)S(1)}, u32[]{:S(2)}, u32[]{:S(2)}) collective-permute-start(bf16[1,12,16,512]{3,2,1,0:T(8,128)(2,1)S(1)} %get-tuple-element.631), channel_id=1, source_target_pairs={{8,0},{16,8},{24,16},{9,1},{17,9},{25,17},{10,2},{18,10},{26,18},{... | collective-permute-start | bytes 589832 | tf_op jit(solution)/shard_map/while/body/eval_jaxpr/ppermute | solution.py:12
  109.9 8.6 %collective-permute-start = (bf16[1,12,16,512]{3,2,1,0:T(8,128)(2,1)S(1)}, bf16[1,12,16,512]{3,2,1,0:T(8,128)(2,1)S(1)}, u32[]{:S(2)}, u32[]{:S(2)}) collective-permute-start(bf16[1,12,16,512]{3,2,1,0:T(8,128)(2,1)S(1)} %get-tuple-element.631), channel_id=1, source_target_pairs={{8,0},{16,8},{24,16},{9,1},{17,9},{25,17},{10,2},{18,10},{26,18},{... | collective-permute-start | bytes 589832 | tf_op jit(solution)/shard_map/while/body/eval_jaxpr/ppermute | solution.py:12
  134.7 8.6 %collective-permute-start = (bf16[1,12,16,512]{3,2,1,0:T(8,128)(2,1)S(1)}, bf16[1,12,16,512]{3,2,1,0:T(8,128)(2,1)S(1)}, u32[]{:S(2)}, u32[]{:S(2)}) collective-permute-start(bf16[1,12,16,512]{3,2,1,0:T(8,128)(2,1)S(1)} %get-tuple-element.631), channel_id=1, source_target_pairs={{8,0},{16,8},{24,16},{9,1},{17,9},{25,17},{10,2},{18,10},{26,18},{... | collective-permute-start | bytes 589832 | tf_op jit(solution)/shard_map/while/body/eval_jaxpr/ppermute | solution.py:12
  159.6 8.6 %collective-permute-start = (bf16[1,12,16,512]{3,2,1,0:T(8,128)(2,1)S(1)}, bf16[1,12,16,512]{3,2,1,0:T(8,128)(2,1)S(1)}, u32[]{:S(2)}, u32[]{:S(2)}) collective-permute-start(bf16[1,12,16,512]{3,2,1,0:T(8,128)(2,1)S(1)} %get-tuple-element.631), channel_id=1, source_target_pairs={{8,0},{16,8},{24,16},{9,1},{17,9},{25,17},{10,2},{18,10},{26,18},{... | collective-permute-start | bytes 589832 | tf_op jit(solution)/shard_map/while/body/eval_jaxpr/ppermute | solution.py:12
  184.4 8.6 %collective-permute-start = (bf16[1,12,16,512]{3,2,1,0:T(8,128)(2,1)S(1)}, bf16[1,12,16,512]{3,2,1,0:T(8,128)(2,1)S(1)}, u32[]{:S(2)}, u32[]{:S(2)}) collective-permute-start(bf16[1,12,16,512]{3,2,1,0:T(8,128)(2,1)S(1)} %get-tuple-element.631), channel_id=1, source_target_pairs={{8,0},{16,8},{24,16},{9,1},{17,9},{25,17},{10,2},{18,10},{26,18},{... | collective-permute-start | bytes 589832 | tf_op jit(solution)/shard_map/while/body/eval_jaxpr/ppermute | solution.py:12
  209.3 8.6 %collective-permute-start = (bf16[1,12,16,512]{3,2,1,0:T(8,128)(2,1)S(1)}, bf16[1,12,16,512]{3,2,1,0:T(8,128)(2,1)S(1)}, u32[]{:S(2)}, u32[]{:S(2)}) collective-permute-start(bf16[1,12,16,512]{3,2,1,0:T(8,128)(2,1)S(1)} %get-tuple-element.631), channel_id=1, source_target_pairs={{8,0},{16,8},{24,16},{9,1},{17,9},{25,17},{10,2},{18,10},{26,18},{... | collective-permute-start | bytes 589832 | tf_op jit(solution)/shard_map/while/body/eval_jaxpr/ppermute | solution.py:12
  217.8 9.4 %copy-start.5 = (f32[512]{0:T(512)}, f32[512]{0:T(512)S(1)}, u32[]{:S(2)}) copy-start(f32[512]{0:T(512)S(1)} %get-tuple-element.371) | copy-start | bytes 6148
  217.8 9.4 %copy-start.7 = (f32[512]{0:T(512)}, f32[512]{0:T(512)S(1)}, u32[]{:S(2)}) copy-start(f32[512]{0:T(512)S(1)} %get-tuple-element.372) | copy-start | bytes 6148
  217.8 3.0 %copy-start = (f32[4,1,12,16,512]{4,3,2,1,0:T(8,128)S(1)}, f32[4,1,12,16,512]{4,3,2,1,0:T(8,128)}, u32[]{:S(2)}) copy-start(f32[4,1,12,16,512]{4,3,2,1,0:T(8,128)} %get-tuple-element.370) | copy-start | bytes 4718596
  217.8 3.0 %copy-start.3 = (bf16[4,1,12,16,512]{4,3,2,1,0:T(8,128)(2,1)S(1)}, bf16[4,1,12,16,512]{4,3,2,1,0:T(8,128)(2,1)}, u32[]{:S(2)}) copy-start(bf16[4,1,12,16,512]{4,3,2,1,0:T(8,128)(2,1)} %get-tuple-element.695) | copy-start | bytes 2359300
Sparse Core Ops, SparseCore 0:
  220.9 53.1 all-reduce.7
where the time goes:
time: 285 us; the launch traced here: 283 us
  blocking collectives  131 us (46%)
  other arithmetic  61.9 us (22%)
  waiting for transfers between devices  49.7 us (17%)
  between operations  14.3 us (5%)
  local copies, waits for them, and re-layouts  10.3 us (4%)
  starting transfers between devices  9 us (3%)
  matrix products  6.9 us (2%)
    psum x7, blocking collectives, step(): lax.psum((jnp.sum(upstream, axis=0), jnp.sum(upstream * normed, axis=0)),...  82.6 us
    ppermute x7, waiting for transfers between devices, shifted(): return lax.ppermute(x, axis, pairs)  26.1 us
    psum x1, blocking collectives, body(): lax.psum((jnp.sum(pre_norm, axis=1), jnp.sum(pre_norm * pre_norm, axis=1)...  25.5 us
    psum x1, waiting for transfers between devices, body(): lax.psum(point_acc.astype(jnp.bfloat16), 'dp').astype(jnp.float32)  23.5 us
    psum x1, blocking collectives, body(): lax.psum(kernel_acc.astype(jnp.bfloat16), 'dp').astype(jnp.float32)  22.5 us
    dynamic_update_slice x7, other arithmetic, step(): grads_out = lax.dynamic_update_index_in_dim(grads_out, kept_grad, slot, 0)  13.9 us
    dynamic_update_slice x7, other arithmetic, step(): lax.dynamic_update_index_in_dim(depth_store, kept_depth, slot, 0)  12.6 us
    dynamic_update_slice x7, other arithmetic, step(): pre_store = lax.dynamic_update_index_in_dim(pre_store, kept_pre, slot, 0)  12.1 us
  transfers between devices with their start and end apart: 8, of which 8 were waited for; matrix products, arithmetic and copies ran while one was open for 11% of the time, Pallas kernels for 0%

commit v1 on v0

--- a/solution.py
+++ b/solution.py
@@ -160,7 +160,7 @@
     )
     point_sum, kernel_sum = (
         lax.psum(point_acc.astype(jnp.bfloat16), "dp").astype(jnp.float32),
-        lax.psum(kernel_acc.astype(jnp.bfloat16), "dp").astype(jnp.float32),
+        jnp.sum(lax.all_gather(kernel_acc.astype(jnp.bfloat16), "dp"), axis=0).astype(jnp.float32),
     )
     return (grads_out[None], point_sum[None], kernel_sum[None], gain_acc[None], bias_acc[None])
 

time: 285 us -> 285 us (level)
  blocking collectives: 131 us -> 116 us
  waiting for transfers between devices: 49.7 us -> 64 us
    psum x1 -> x0, blocking collectives: 22.5 us -> none  [body(): lax.psum(kernel_acc.astype(jnp.bfloat16), 'dp').astype(jnp.float32)]
    psum x1, waiting for transfers between devices: 23.5 us -> 37.9 us  [body(): lax.psum(point_acc.astype(jnp.bfloat16), 'dp').astype(jnp.float32)]
    all_gather x0 -> x1, blocking collectives: none -> 8.27 us  [body(): lax.all_gather(kernel_acc.astype(jnp.bfloat16), 'dp')]
where the time goes in v1:
time: 285 us; the launch traced here: 283 us
  blocking collectives  116 us (41%)
  waiting for transfers between devices  64 us (22%)
  other arithmetic  61.4 us (22%)
  between operations  14.3 us (5%)
  local copies, waits for them, and re-layouts  10.9 us (4%)
  starting transfers between devices  9 us (3%)
  matrix products  6.9 us (2%)
    psum x7, blocking collectives, step(): lax.psum((jnp.sum(upstream, axis=0), jnp.sum(upstream * normed, axis=0)),...  82.6 us
    psum x1, waiting for transfers between devices, body(): lax.psum(point_acc.astype(jnp.bfloat16), 'dp').astype(jnp.float32)  37.9 us
    ppermute x7, waiting for transfers between devices, shifted(): return lax.ppermute(x, axis, pairs)  26.1 us
    psum x1, blocking collectives, body(): lax.psum((jnp.sum(pre_norm, axis=1), jnp.sum(pre_norm * pre_norm, axis=1)...  25.5 us
    dynamic_update_slice x7, other arithmetic, step(): grads_out = lax.dynamic_update_index_in_dim(grads_out, kept_grad, slot, 0)  13.9 us
    dynamic_update_slice x7, other arithmetic, step(): lax.dynamic_update_index_in_dim(depth_store, kept_depth, slot, 0)  12.6 us
    dynamic_update_slice x7, other arithmetic, step(): pre_store = lax.dynamic_update_index_in_dim(pre_store, kept_pre, slot, 0)  12.1 us
    ppermute x7, starting transfers between devices, shifted(): return lax.ppermute(x, axis, pairs)  8.96 us
  transfers between devices with their start and end apart: 8, of which 8 were waited for; matrix products, arithmetic and copies ran while one was open for 11% of the time, Pallas kernels for 0%

profile of v1, /device:TPU:0, one launch (start us, length us, event | category | flops | bytes accessed | tf_op | source)
XLA Modules:
  0.0 283.2 jit_solution(156822704427930493)
XLA Ops:
  9.3 2.2 add_convert_fusion
  13.3 25.5 %all-reduce.3 = (f32[4,512]{1,0:T(4,128)S(1)}, f32[4,512]{1,0:T(4,128)S(1)}) all-reduce(f32[4,512]{1,0:T(4,128)S(1)} %get-tuple-element.436, f32[4,512]{1,0:T(4,128)S(1)} %get-tuple-element.435), channel_id=1, replica_groups=mesh['section'=4,'dp'=8] {'dp'}, use_global_device_ids=true, to_apply=%region_3.4 | all-reduce | flops 4096 | bytes 32768 | tf_op jit(solution)/shard_map/psum | solution.py:84
  43.9 174.0 %while.26 = (s32[]{:T(128)}, bf16[1,12,16,512]{3,2,1,0:T(8,128)(2,1)S(1)}, bf16[4,1,12,16,512]{4,3,2,1,0:T(8,128)(2,1)}, f32[512]{0:T(512)S(1)}, f32[512]{0:T(51...) while((s32[]{:T(128)}, ...), condition=%wide.region_9.10_spmd.clone, body=%wide.region_4.9_spmd.clone.sunk | while | flops 105189384 | bytes 8489298 | solution.py:149
  46.0 11.8 %all-reduce.5 = (f32[512]{0:T(512)S(1)}, f32[512]{0:T(512)S(1)}) all-reduce(f32[512]{0:T(512)S(1)} %get-tuple-element.621, f32[512]{0:T(512)S(1)} %get-tuple-element.622), channel_id=1, replica_groups=mesh['section'=4,'dp'=8] {'dp'}, use_global_device_ids=true, to_apply=%region_8.8 | all-reduce | flops 1024 | bytes 8192 | tf_op jit(solution)/shard_map/while/body/eval_jaxpr/psum | solution.py:105
  58.2 2.0 bitcast_dynamic-update-slice_fusion.2
  65.0 3.7 %collective-permute-done = bf16[1,12,16,512]{3,2,1,0:T(8,128)(2,1)S(1)} collective-permute-done((bf16[1,12,16,512]{3,2,1,0:T(8,128)(2,1)S(1)}, bf16[1,12,16,512]{3,2,1,0:T(8,128)(2,1)S(1)}, u32[]{:S(2)}, u32[]{:S(2)}) %collective-permute-start) | collective-permute-done | bytes 196640 | tf_op jit(solution)/shard_map/while/body/eval_jaxpr/ppermute | solution.py:12
  70.8 11.8 %all-reduce.5 = (f32[512]{0:T(512)S(1)}, f32[512]{0:T(512)S(1)}) all-reduce(f32[512]{0:T(512)S(1)} %get-tuple-element.621, f32[512]{0:T(512)S(1)} %get-tuple-element.622), channel_id=1, replica_groups=mesh['section'=4,'dp'=8] {'dp'}, use_global_device_ids=true, to_apply=%region_8.8 | all-reduce | flops 1024 | bytes 8192 | tf_op jit(solution)/shard_map/while/body/eval_jaxpr/psum | solution.py:105
  89.8 3.7 %collective-permute-done = bf16[1,12,16,512]{3,2,1,0:T(8,128)(2,1)S(1)} collective-permute-done((bf16[1,12,16,512]{3,2,1,0:T(8,128)(2,1)S(1)}, bf16[1,12,16,512]{3,2,1,0:T(8,128)(2,1)S(1)}, u32[]{:S(2)}, u32[]{:S(2)}) %collective-permute-start) | collective-permute-done | bytes 196640 | tf_op jit(solution)/shard_map/while/body/eval_jaxpr/ppermute | solution.py:12
  95.7 11.8 %all-reduce.5 = (f32[512]{0:T(512)S(1)}, f32[512]{0:T(512)S(1)}) all-reduce(f32[512]{0:T(512)S(1)} %get-tuple-element.621, f32[512]{0:T(512)S(1)} %get-tuple-element.622), channel_id=1, replica_groups=mesh['section'=4,'dp'=8] {'dp'}, use_global_device_ids=true, to_apply=%region_8.8 | all-reduce | flops 1024 | bytes 8192 | tf_op jit(solution)/shard_map/while/body/eval_jaxpr/psum | solution.py:105
  107.9 2.0 bitcast_dynamic-update-slice_fusion.2
  114.7 3.7 %collective-permute-done = bf16[1,12,16,512]{3,2,1,0:T(8,128)(2,1)S(1)} collective-permute-done((bf16[1,12,16,512]{3,2,1,0:T(8,128)(2,1)S(1)}, bf16[1,12,16,512]{3,2,1,0:T(8,128)(2,1)S(1)}, u32[]{:S(2)}, u32[]{:S(2)}) %collective-permute-start) | collective-permute-done | bytes 196640 | tf_op jit(solution)/shard_map/while/body/eval_jaxpr/ppermute | solution.py:12
  120.5 11.8 %all-reduce.5 = (f32[512]{0:T(512)S(1)}, f32[512]{0:T(512)S(1)}) all-reduce(f32[512]{0:T(512)S(1)} %get-tuple-element.621, f32[512]{0:T(512)S(1)} %get-tuple-element.622), channel_id=1, replica_groups=mesh['section'=4,'dp'=8] {'dp'}, use_global_device_ids=true, to_apply=%region_8.8 | all-reduce | flops 1024 | bytes 8192 | tf_op jit(solution)/shard_map/while/body/eval_jaxpr/psum | solution.py:105
  139.5 3.7 %collective-permute-done = bf16[1,12,16,512]{3,2,1,0:T(8,128)(2,1)S(1)} collective-permute-done((bf16[1,12,16,512]{3,2,1,0:T(8,128)(2,1)S(1)}, bf16[1,12,16,512]{3,2,1,0:T(8,128)(2,1)S(1)}, u32[]{:S(2)}, u32[]{:S(2)}) %collective-permute-start) | collective-permute-done | bytes 196640 | tf_op jit(solution)/shard_map/while/body/eval_jaxpr/ppermute | solution.py:12
  145.4 11.8 %all-reduce.5 = (f32[512]{0:T(512)S(1)}, f32[512]{0:T(512)S(1)}) all-reduce(f32[512]{0:T(512)S(1)} %get-tuple-element.621, f32[512]{0:T(512)S(1)} %get-tuple-element.622), channel_id=1, replica_groups=mesh['section'=4,'dp'=8] {'dp'}, use_global_device_ids=true, to_apply=%region_8.8 | all-reduce | flops 1024 | bytes 8192 | tf_op jit(solution)/shard_map/while/body/eval_jaxpr/psum | solution.py:105
  164.4 3.7 %collective-permute-done = bf16[1,12,16,512]{3,2,1,0:T(8,128)(2,1)S(1)} collective-permute-done((bf16[1,12,16,512]{3,2,1,0:T(8,128)(2,1)S(1)}, bf16[1,12,16,512]{3,2,1,0:T(8,128)(2,1)S(1)}, u32[]{:S(2)}, u32[]{:S(2)}) %collective-permute-start) | collective-permute-done | bytes 196640 | tf_op jit(solution)/shard_map/while/body/eval_jaxpr/ppermute | solution.py:12
  170.2 11.8 %all-reduce.5 = (f32[512]{0:T(512)S(1)}, f32[512]{0:T(512)S(1)}) all-reduce(f32[512]{0:T(512)S(1)} %get-tuple-element.621, f32[512]{0:T(512)S(1)} %get-tuple-element.622), channel_id=1, replica_groups=mesh['section'=4,'dp'=8] {'dp'}, use_global_device_ids=true, to_apply=%region_8.8 | all-reduce | flops 1024 | bytes 8192 | tf_op jit(solution)/shard_map/while/body/eval_jaxpr/psum | solution.py:105
  189.2 3.7 %collective-permute-done = bf16[1,12,16,512]{3,2,1,0:T(8,128)(2,1)S(1)} collective-permute-done((bf16[1,12,16,512]{3,2,1,0:T(8,128)(2,1)S(1)}, bf16[1,12,16,512]{3,2,1,0:T(8,128)(2,1)S(1)}, u32[]{:S(2)}, u32[]{:S(2)}) %collective-permute-start) | collective-permute-done | bytes 196640 | tf_op jit(solution)/shard_map/while/body/eval_jaxpr/ppermute | solution.py:12
  195.1 11.8 %all-reduce.5 = (f32[512]{0:T(512)S(1)}, f32[512]{0:T(512)S(1)}) all-reduce(f32[512]{0:T(512)S(1)} %get-tuple-element.621, f32[512]{0:T(512)S(1)} %get-tuple-element.622), channel_id=1, replica_groups=mesh['section'=4,'dp'=8] {'dp'}, use_global_device_ids=true, to_apply=%region_8.8 | all-reduce | flops 1024 | bytes 8192 | tf_op jit(solution)/shard_map/while/body/eval_jaxpr/psum | solution.py:105
  214.1 3.7 %collective-permute-done = bf16[1,12,16,512]{3,2,1,0:T(8,128)(2,1)S(1)} collective-permute-done((bf16[1,12,16,512]{3,2,1,0:T(8,128)(2,1)S(1)}, bf16[1,12,16,512]{3,2,1,0:T(8,128)(2,1)S(1)}, u32[]{:S(2)}, u32[]{:S(2)}) %collective-permute-start) | collective-permute-done | bytes 196640 | tf_op jit(solution)/shard_map/while/body/eval_jaxpr/ppermute | solution.py:12
  217.8 2.9 %fusion.37 = bf16[1,512,512]{2,1,0:T(8,128)(2,1)} fusion(bf16[768,512]{1,0:T(8,128)(2,1)} %bitcast.175, bf16[768,512]{1,0:T(8,128)(2,1)} %bitcast.173), kind=kOutput, calls=%fused_computation.83 | convolution fusion | flops 402915328 | bytes 2097152 | tf_op jit(solution)/shard_map/dot_general | solution.py:151
  220.8 6.4 %fusion.28 = (bf16[512]{0:T(512)(128)(2,1)S(1)}, bf16[512]{0:T(512)(128)(2,1)S(1)}, bf16[512]{0:T(512)(128)(2,1)S(1)}, bf16[512]{0:T(512)(128)(2,1)S(1)}, bf16[5...) fusion(f32[4,1,12,16,512]{4,3,2,1,0:T(8,128)S(1)} %copy-done, ...), kind=kLoop, calls=%fused_computation.69 | loop fusion | flops 7859712 | bytes 3941376 | tf_op jit(solution)/shard_map/reduce_sum | solution.py:51
  227.4 8.3 %all_gather.4 = bf16[8,3,3,512]{3,2,1,0:T(4,128)(2,1)S(1)} all-gather(bf16[1,3,3,512]{3,2,1,0:T(4,128)(2,1)S(1)} %pad_maximum_fusion), channel_id=1, replica_groups=mesh['section'=4,'dp'=8] {'dp'}, dimensions={0}, use_global_device_ids=true | all-gather | bytes 82944 | tf_op jit(solution)/shard_map/all_gather | solution.py:163
  236.3 37.9 %all-reduce.8.cloned.1.call-done = bf16[1,512,512]{2,1,0:T(8,128)(2,1)} async-done(((bf16[1,512,512]{2,1,0:T(8,128)(2,1)}), bf16[1,512,512]{2,1,0:T(8,128)(2,1)}) %all-reduce.8.cloned.1.call-update) | async-done | bytes 524304 | tf_op jit(solution)/shard_map/psum | solution.py:162
  274.2 2.1 broadcast_in_dim.67
  (133 shorter events, 70.6 us)
Async XLA Ops:
  7.2 267.0 %all-reduce.8.cloned.1.call-start = ((), (), s32[]{:S(2)}) async-start(), calls=%async_computation | async-start | bytes 1048576 | tf_op jit(solution)/shard_map/psum | solution.py:162
  9.3 4.0 %copy-start.1 = (f32[4,12,16,512]{3,2,1,0:T(8,128)}, f32[4,12,16,512]{3,2,1,0:T(8,128)S(1)}, u32[]{:S(2)}) copy-start(f32[4,12,16,512]{3,2,1,0:T(8,128)S(1)} %maximum_bitcast_fusion) | copy-start | bytes 4718596
  9.3 2.2 copy-start.2
  11.6 1.8 copy-start.4
  40.6 3.3 %copy-start.6 = (f32[1,512]{1,0:T(1,128)S(1)}, f32[1,512]{1,0:T(1,128)}, u32[]{:S(2)}) copy-start(f32[1,512]{1,0:T(1,128)} %param.11) | copy-start | bytes 6148
  60.2 8.6 %collective-permute-start = (bf16[1,12,16,512]{3,2,1,0:T(8,128)(2,1)S(1)}, bf16[1,12,16,512]{3,2,1,0:T(8,128)(2,1)S(1)}, u32[]{:S(2)}, u32[]{:S(2)}) collective-permute-start(bf16[1,12,16,512]{3,2,1,0:T(8,128)(2,1)S(1)} %get-tuple-element.631), channel_id=1, source_target_pairs={{8,0},{16,8},{24,16},{9,1},{17,9},{25,17},{10,2},{18,10},{26,18},{... | collective-permute-start | bytes 589832 | tf_op jit(solution)/shard_map/while/body/eval_jaxpr/ppermute | solution.py:12
  85.0 8.6 %collective-permute-start = (bf16[1,12,16,512]{3,2,1,0:T(8,128)(2,1)S(1)}, bf16[1,12,16,512]{3,2,1,0:T(8,128)(2,1)S(1)}, u32[]{:S(2)}, u32[]{:S(2)}) collective-permute-start(bf16[1,12,16,512]{3,2,1,0:T(8,128)(2,1)S(1)} %get-tuple-element.631), channel_id=1, source_target_pairs={{8,0},{16,8},{24,16},{9,1},{17,9},{25,17},{10,2},{18,10},{26,18},{... | collective-permute-start | bytes 589832 | tf_op jit(solution)/shard_map/while/body/eval_jaxpr/ppermute | solution.py:12
  109.9 8.6 %collective-permute-start = (bf16[1,12,16,512]{3,2,1,0:T(8,128)(2,1)S(1)}, bf16[1,12,16,512]{3,2,1,0:T(8,128)(2,1)S(1)}, u32[]{:S(2)}, u32[]{:S(2)}) collective-permute-start(bf16[1,12,16,512]{3,2,1,0:T(8,128)(2,1)S(1)} %get-tuple-element.631), channel_id=1, source_target_pairs={{8,0},{16,8},{24,16},{9,1},{17,9},{25,17},{10,2},{18,10},{26,18},{... | collective-permute-start | bytes 589832 | tf_op jit(solution)/shard_map/while/body/eval_jaxpr/ppermute | solution.py:12
  134.7 8.6 %collective-permute-start = (bf16[1,12,16,512]{3,2,1,0:T(8,128)(2,1)S(1)}, bf16[1,12,16,512]{3,2,1,0:T(8,128)(2,1)S(1)}, u32[]{:S(2)}, u32[]{:S(2)}) collective-permute-start(bf16[1,12,16,512]{3,2,1,0:T(8,128)(2,1)S(1)} %get-tuple-element.631), channel_id=1, source_target_pairs={{8,0},{16,8},{24,16},{9,1},{17,9},{25,17},{10,2},{18,10},{26,18},{... | collective-permute-start | bytes 589832 | tf_op jit(solution)/shard_map/while/body/eval_jaxpr/ppermute | solution.py:12
  159.6 8.6 %collective-permute-start = (bf16[1,12,16,512]{3,2,1,0:T(8,128)(2,1)S(1)}, bf16[1,12,16,512]{3,2,1,0:T(8,128)(2,1)S(1)}, u32[]{:S(2)}, u32[]{:S(2)}) collective-permute-start(bf16[1,12,16,512]{3,2,1,0:T(8,128)(2,1)S(1)} %get-tuple-element.631), channel_id=1, source_target_pairs={{8,0},{16,8},{24,16},{9,1},{17,9},{25,17},{10,2},{18,10},{26,18},{... | collective-permute-start | bytes 589832 | tf_op jit(solution)/shard_map/while/body/eval_jaxpr/ppermute | solution.py:12
  184.4 8.6 %collective-permute-start = (bf16[1,12,16,512]{3,2,1,0:T(8,128)(2,1)S(1)}, bf16[1,12,16,512]{3,2,1,0:T(8,128)(2,1)S(1)}, u32[]{:S(2)}, u32[]{:S(2)}) collective-permute-start(bf16[1,12,16,512]{3,2,1,0:T(8,128)(2,1)S(1)} %get-tuple-element.631), channel_id=1, source_target_pairs={{8,0},{16,8},{24,16},{9,1},{17,9},{25,17},{10,2},{18,10},{26,18},{... | collective-permute-start | bytes 589832 | tf_op jit(solution)/shard_map/while/body/eval_jaxpr/ppermute | solution.py:12
  209.3 8.6 %collective-permute-start = (bf16[1,12,16,512]{3,2,1,0:T(8,128)(2,1)S(1)}, bf16[1,12,16,512]{3,2,1,0:T(8,128)(2,1)S(1)}, u32[]{:S(2)}, u32[]{:S(2)}) collective-permute-start(bf16[1,12,16,512]{3,2,1,0:T(8,128)(2,1)S(1)} %get-tuple-element.631), channel_id=1, source_target_pairs={{8,0},{16,8},{24,16},{9,1},{17,9},{25,17},{10,2},{18,10},{26,18},{... | collective-permute-start | bytes 589832 | tf_op jit(solution)/shard_map/while/body/eval_jaxpr/ppermute | solution.py:12
  217.8 9.4 %copy-start.5 = (f32[512]{0:T(512)}, f32[512]{0:T(512)S(1)}, u32[]{:S(2)}) copy-start(f32[512]{0:T(512)S(1)} %get-tuple-element.371) | copy-start | bytes 6148
  217.8 9.4 %copy-start.7 = (f32[512]{0:T(512)}, f32[512]{0:T(512)S(1)}, u32[]{:S(2)}) copy-start(f32[512]{0:T(512)S(1)} %get-tuple-element.372) | copy-start | bytes 6148
  217.8 3.0 %copy-start = (f32[4,1,12,16,512]{4,3,2,1,0:T(8,128)S(1)}, f32[4,1,12,16,512]{4,3,2,1,0:T(8,128)}, u32[]{:S(2)}) copy-start(f32[4,1,12,16,512]{4,3,2,1,0:T(8,128)} %get-tuple-element.370) | copy-start | bytes 4718596
  217.8 3.0 %copy-start.3 = (bf16[4,1,12,16,512]{4,3,2,1,0:T(8,128)(2,1)S(1)}, bf16[4,1,12,16,512]{4,3,2,1,0:T(8,128)(2,1)}, u32[]{:S(2)}) copy-start(bf16[4,1,12,16,512]{4,3,2,1,0:T(8,128)(2,1)} %get-tuple-element.695) | copy-start | bytes 2359300
Sparse Core Ops, SparseCore 0:
  220.9 53.2 all-reduce.7
